TPU v7x, 128 devices: a whole 4x4x4 slice. The times are simulated.
128 devices in a mesh: freq: 16 (over x, z_lo, core), src: 8 (over y, z_hi).
Axes of the slice: x: 4, y: 4, z: 4 (z_hi: 2, z_lo: 2; z = z_hi * 2 + z_lo), core: 2. Of those that a mesh axis runs over, the one named last changes fastest.
Arguments:
- focusing: bfloat16 [64, 1024, 2048], P('src', 'freq'), may hold values from -6 to 6
- direct: bfloat16 [64, 1024, 2048], P('src', 'freq'), may hold values from -6 to 6
- kernel: bfloat16 [2, 192, 2048, 1024], P(None, 'freq', 'src'), may hold values from -0.125 to 0.125
- onset_up: int32 [64, 2048], P('freq', 'src'), may hold values from 256 to 2048
- onset_back: int32 [64, 1024], P('src', 'freq'), may hold values from 256 to 2048
Outputs:
- upgoing: bfloat16 [64, 2048, 2048], P('freq', 'src')
- updated: bfloat16 [64, 1024, 2048], P('src', 'freq')
All inputs are finite; a program needn't handle non-finite values.
Results may differ from a plain program's by a relative error of at most 0.008.
Values may be sent and summed in bfloat16 or wider, within the bound.
No kernel may reach another device: no remote copies, remote signals or barrier semaphores. Data moves between devices by JAX's collectives and lax.ppermute only.
A program may use at most 128 MiB of HBM per device.

v0:
```python
import math
import jax
import jax.numpy as jnp
from jax import lax
from jax.sharding import PartitionSpec as P

NT = 2048
NF = 192
BIN0 = 16


def frequency_band_tables():
    sample_index = jnp.arange(NT, dtype=jnp.int32)
    bin_index = BIN0 + jnp.arange(NF, dtype=jnp.int32)
    phase = sample_index[:, None] * bin_index[None, :] % NT
    angle = phase.astype(jnp.float32) * (2.0 * math.pi / NT)
    cosine = jnp.cos(angle)
    sine = jnp.sin(angle)
    forward_table = jnp.stack([cosine, -sine], axis=2).reshape(NT, 2 * NF).astype(jnp.bfloat16)
    inverse_table = (
        (2.0 / NT * jnp.stack([cosine.T, -sine.T], axis=1)).reshape(2 * NF, NT).astype(jnp.bfloat16)
    )
    return (forward_table, inverse_table)


def forward_waves(kernel_real_part, kernel_imaginary, spectrum):
    spectral_real = spectrum[:, 0]
    spectral_imaginary = spectrum[:, 1]
    wave_real = jnp.einsum(
        "izb,ijb->ijz", kernel_real_part, spectral_real, preferred_element_type=jnp.float32
    ) - jnp.einsum(
        "izb,ijb->ijz", kernel_imaginary, spectral_imaginary, preferred_element_type=jnp.float32
    )
    wave_imag = jnp.einsum(
        "izb,ijb->ijz", kernel_real_part, spectral_imaginary, preferred_element_type=jnp.float32
    ) + jnp.einsum(
        "izb,ijb->ijz", kernel_imaginary, spectral_real, preferred_element_type=jnp.float32
    )
    return jnp.stack([wave_real, wave_imag], axis=1).astype(jnp.bfloat16)


def adjoint_terms(kernel_real_part, kernel_imaginary, spectrum):
    backward_real = spectrum[:, 0]
    backward_imaginary = spectrum[:, 1]
    term_real = jnp.einsum(
        "doy,dvo->vdy", kernel_real_part, backward_real, preferred_element_type=jnp.float32
    ) + jnp.einsum(
        "doy,dvo->vdy", kernel_imaginary, backward_imaginary, preferred_element_type=jnp.float32
    )
    term_imag = jnp.einsum(
        "doy,dvo->vdy", kernel_real_part, backward_imaginary, preferred_element_type=jnp.float32
    ) - jnp.einsum(
        "doy,dvo->vdy", kernel_imaginary, backward_real, preferred_element_type=jnp.float32
    )
    return jnp.stack([term_real, term_imag], axis=2)


def local(focusing, direct, kernel, onset_up, onset_back):
    forward_table, inverse_table = frequency_band_tables()
    kernel_real_part = kernel[0]
    kernel_imaginary = kernel[1]
    sample_index = jnp.arange(NT, dtype=jnp.int32)
    point_count = focusing.shape[0]
    recv_count = focusing.shape[1]
    bins_local = jnp.einsum(
        "tk,prt->kpr", forward_table, focusing, preferred_element_type=jnp.float32
    )
    bins_local = bins_local.astype(jnp.bfloat16).reshape(NF, 2, point_count, recv_count)
    everyone = lax.all_gather(bins_local, "src", axis=2, tiled=True)
    waves = forward_waves(
        kernel_real_part,
        kernel_imaginary,
        lax.all_to_all(everyone, "freq", split_axis=0, concat_axis=3, tiled=True),
    )
    timed = lax.all_to_all(waves, "freq", split_axis=2, concat_axis=0, tiled=True)
    up_points = timed.shape[2]
    source_count = timed.shape[3]
    signal = jnp.einsum(
        "kps,kt->pst",
        timed.reshape(2 * NF, up_points, source_count),
        inverse_table,
        preferred_element_type=jnp.float32,
    )
    upgoing = jnp.where(sample_index[None, None, :] < onset_up[:, :, None], signal, 0.0).astype(
        jnp.bfloat16
    )
    back_local = jnp.einsum(
        "tk,pst->kps", forward_table, upgoing, preferred_element_type=jnp.float32
    )
    back_local = back_local.astype(jnp.bfloat16).reshape(NF, 2, up_points, source_count)
    banded = lax.all_to_all(back_local, "freq", split_axis=0, concat_axis=2, tiled=True)
    partial_terms = adjoint_terms(kernel_real_part, kernel_imaginary, banded).astype(jnp.bfloat16)
    moved = lax.all_to_all(partial_terms, "freq", split_axis=3, concat_axis=1, tiled=True)
    summed = (
        lax.psum_scatter(moved, "src", scatter_dimension=0, tiled=True)
        .astype(jnp.float32)
        .astype(jnp.bfloat16)
    )
    back_count = summed.shape[3]
    trace = jnp.einsum(
        "pkr,kt->prt",
        summed.reshape(point_count, 2 * NF, back_count),
        inverse_table,
        preferred_element_type=jnp.float32,
    )
    cut = jnp.where(sample_index[None, None, :] < onset_back[:, :, None], trace, 0.0)
    updated = (direct.astype(jnp.float32) - cut).astype(jnp.bfloat16)
    return (upgoing, updated)


def solution(mesh):
    placed = (
        P("src", "freq", None),
        P("src", "freq", None),
        P(None, "freq", "src", None),
        P("freq", "src"),
        P("src", "freq"),
    )
    return jax.shard_map(
        local,
        mesh=mesh,
        in_specs=placed,
        out_specs=(P("freq", "src", None), P("src", "freq", None)),
        check_vma=False,
    )
```

profile of v0, /device:TPU:0, one launch (start us, length us, event | category | flops | bytes accessed | tf_op | source)
XLA Modules:
  0.0 504.8 jit_solution(12992001424295173069)
XLA Ops:
  7.2 6.9 %cosine_convert_fusion = (bf16[2048,192,1]{0,1,2:T(8,128)(2,1)S(1)}, bf16[2048,192,1]{0,1,2:T(8,128)(2,1)S(1)}) fusion(s32[192]{0:T(256)S(1)} %iota_add_fusion), kind=kLoop, calls=%fused_computation.57 | loop fusion | flops 6684672 | bytes 1573632 | tf_op jit(solution)/shard_map/convert.10
  24.8 101.0 %all-gather.2.cloned.1.call-done = bf16[192,2,64,64]{3,2,1,0:T(8,128)(2,1)} async-done(((bf16[192,2,8,64]{3,2,1,0:T(8,128)(2,1)}), bf16[192,2,64,64]{3,2,1,0:T(8,128)(2,1)}) %all-gather.2.cloned.1.call-update) | async-done | bytes 3145744 | tf_op jit(solution)/shard_map/all_gather | solution.py:69
  125.8 12.7 %reshape.241 = bf16[16,2,49152]{2,1,0:T(2,128)(2,1)} reshape(bf16[192,2,64,64]{3,2,1,0:T(8,128)(2,1)} %all-gather.2.cloned.1.call-done) | data formatting | bytes 6291456
  138.5 4.9 all-to-all-start
  145.4 37.0 %all-to-all-done = bf16[16,2,49152]{2,1,0:T(2,128)(2,1)} async-done(((bf16[16,2,49152]{2,1,0:T(2,128)(2,1)}), bf16[16,2,49152]{2,1,0:T(2,128)(2,1)}, u32[]{:S(2)}, u32[]{:S(2)}) %all-to-all-start) | async-done | bytes 3145760 | tf_op jit(solution)/shard_map/all_to_all | solution.py:73
  182.4 12.3 %reshape.242 = bf16[192,2,64,64]{3,2,1,0:T(8,128)(2,1)} reshape(bf16[16,2,49152]{2,1,0:T(2,128)(2,1)} %all-to-all-done) | data formatting | bytes 6291456
  194.7 11.1 %copy.49 = bf16[12,2,64,16,64]{4,3,2,0,1:T(8,128)(2,1)} copy(bf16[12,2,64,16,64]{4,2,1,0,3:T(8,128)(2,1)} %bitcast.132) | data formatting | bytes 6291456 | tf_op jit(solution)/shard_map/all_to_all | solution.py:73
  205.8 9.9 %all_to_all.53 = bf16[12,2,64,1024]{3,2,0,1:T(8,128)(2,1)} reshape(bf16[12,2,64,16,64]{4,3,2,0,1:T(8,128)(2,1)} %copy.49) | data formatting | bytes 6291456 | tf_op jit(solution)/shard_map/all_to_all | solution.py:73
  215.7 5.4 %fusion.4 = f32[12,64,256]{2,1,0:T(8,128)S(1)} fusion(bf16[2,12,256,1024]{3,2,1,0:T(8,128)(2,1)} %param.7, bf16[12,2,64,1024]{3,2,0,1:T(8,128)(2,1)} %all_to_all.53), kind=kOutput, calls=%fused_computation.6 | convolution fusion | flops 402653184 | bytes 8650752 | tf_op jit(solution)/shard_map/izb,ijb->ijz/dot_general | solution.py:36
  221.2 5.0 fusion.6
  226.2 5.0 fusion.70
  235.1 8.9 %all-to-all-start.1 = ((bf16[12,2,64,256]{3,1,0,2:T(2,128)(2,1)}), bf16[12,2,64,256]{3,1,0,2:T(2,128)(2,1)S(1)}, u32[]{:S(2)}, u32[]{:S(2)}) async-start(bf16[12,2,64,256]{3,1,0,2:T(2,128)(2,1)} %copy.50), calls=%async_computation.1 | async-start | bytes 1572864 | tf_op jit(solution)/shard_map/all_to_all | solution.py:75
  244.2 6.2 %fusion.74 = (f32[192,1,2048]{2,0,1:T(8,128)S(1)}, f32[192,1,2048]{2,0,1:T(8,128)S(1)}) fusion(s32[192]{0:T(256)S(1)} %iota_add_fusion), kind=kLoop, calls=%fused_computation.75 | loop fusion | flops 5898240 | bytes 3146496 | tf_op jit(solution)/shard_map/cos | solution.py:17
  266.7 16.9 %all_to_all.69 = bf16[192,2,4,256]{3,1,2,0:T(2,128)(2,1)S(1)} all-to-all(bf16[192,2,4,256]{3,1,2,0:T(2,128)(2,1)S(1)} %copy.54), channel_id=1, replica_groups=mesh['freq'=16,'src'=8] {'freq'}, dimensions={0} | all-to-all | bytes 1572864 | tf_op jit(solution)/shard_map/all_to_all | solution.py:91
  288.4 4.1 fusion.2
  292.5 4.2 fusion.49
  300.0 15.9 %copy.56 = bf16[64,12,2,1024]{0,2,1,3:T(2,128)(2,1)} copy(bf16[64,12,2,1024]{3,0,1,2:T(8,128)(2,1)} %pad_maximum_fusion) | data formatting | bytes 6291456 | tf_op jit(solution)/shard_map/stack | solution.py:55
  315.9 12.7 %reshape.243 = bf16[16,2,49152]{2,1,0:T(2,128)(2,1)} reshape(bf16[1024,12,2,64]{3,2,1,0:T(2,128)(2,1)} %bitcast.133) | data formatting | bytes 6291456
  328.6 43.4 %all_to_all.70 = bf16[16,2,49152]{2,1,0:T(2,128)(2,1)} all-to-all(bf16[16,2,49152]{2,1,0:T(2,128)(2,1)} %reshape.243), channel_id=1, replica_groups=mesh['freq'=16,'src'=8] {'freq'}, dimensions={0} | all-to-all | bytes 6291456 | tf_op jit(solution)/shard_map/all_to_all | solution.py:93
  372.0 12.3 %reshape.244 = bf16[1024,12,2,64]{3,2,1,0:T(2,128)(2,1)} reshape(bf16[16,2,49152]{2,1,0:T(2,128)(2,1)} %all_to_all.70) | data formatting | bytes 6291456
  384.4 16.3 %copy.57 = bf16[64,12,2,16,64]{4,0,2,1,3:T(8,128)(2,1)} copy(bf16[64,12,2,16,64]{0,2,1,4,3:T(2,128)(2,1)} %bitcast.134) | data formatting | bytes 6291456 | tf_op jit(solution)/shard_map/all_to_all | solution.py:93
  400.7 9.1 %copy.58 = bf16[64,192,2,64]{1,3,2,0:T(8,128)(2,1)} copy(bf16[64,192,2,64]{3,0,2,1:T(8,128)(2,1)} %bitcast.135) | data formatting | bytes 6291456 | tf_op jit(solution)/shard_map/all_to_all | solution.py:93
  409.8 82.9 %reduce-scatter.2.cloned.1.call-done = bf16[8,192,2,64]{1,3,2,0:T(8,128)(2,1)} async-done(((bf16[64,192,2,64]{1,3,2,0:T(8,128)(2,1)}), bf16[8,192,2,64]{1,3,2,0:T(8,128)(2,1)}) %reduce-scatter.2.cloned.1.call-update) | async-done | bytes 393232 | tf_op jit(solution)/shard_map/reduce_scatter | solution.py:95
  492.7 5.0 fusion.17
  (60 shorter events, 40.9 us)
Async XLA Ops:
  7.2 13.6 %copy-start = (bf16[8,64,2048]{2,1,0:T(8,128)(2,1)S(1)}, bf16[8,64,2048]{2,1,0:T(8,128)(2,1)}, u32[]{:S(2)}) copy-start(bf16[8,64,2048]{2,1,0:T(8,128)(2,1)} %param.5) | copy-start | bytes 6291460
  7.2 118.6 %all-gather.2.cloned.1.call-start = ((), (), s32[]{:S(2)}) async-start(), calls=%async_computation.5 | async-start | bytes 7077888 | tf_op jit(solution)/shard_map/all_gather | solution.py:69
  138.5 4.9 copy-start.2
  138.5 43.9 %all-to-all-start = ((bf16[16,2,49152]{2,1,0:T(2,128)(2,1)}), bf16[16,2,49152]{2,1,0:T(2,128)(2,1)}, u32[]{:S(2)}, u32[]{:S(2)}) async-start(bf16[16,2,49152]{2,1,0:T(2,128)(2,1)} %reshape.241), calls=%async_computation | async-start | bytes 6291456 | tf_op jit(solution)/shard_map/all_to_all | solution.py:73
  215.7 5.5 %copy-start.4 = (bf16[12,2,64,1024]{3,2,0,1:T(8,128)(2,1)S(1)}, bf16[12,2,64,1024]{3,2,0,1:T(8,128)(2,1)}, u32[]{:S(2)}) copy-start(bf16[12,2,64,1024]{3,2,0,1:T(8,128)(2,1)} %all_to_all.53) | copy-start | bytes 9437188
  215.7 15.5 %slice-start = ((s8[12582912]{0:T(1024)(128)(4,1)}), s8[4194304]{0:T(1024)(128)(4,1)S(1)}, s32[]{:S(2)}) async-start(s8[12582912]{0:T(1024)(128)(4,1)} %bitcast.128), calls=%async_computation.7 | async-start | bytes 8388608
  221.2 10.1 %slice-start.1 = ((s8[12582912]{0:T(1024)(128)(4,1)}), s8[4194304]{0:T(1024)(128)(4,1)S(1)}, s32[]{:S(2)}) async-start(s8[12582912]{0:T(1024)(128)(4,1)} %bitcast.128), calls=%async_computation.8 | async-start | bytes 8388608
  226.2 5.1 %slice-start.2 = ((s8[12582912]{0:T(1024)(128)(4,1)}), s8[4194304]{0:T(1024)(128)(4,1)S(1)}, s32[]{:S(2)}) async-start(s8[12582912]{0:T(1024)(128)(4,1)} %bitcast.128), calls=%async_computation.9 | async-start | bytes 8388608
  235.1 22.5 %all-to-all-start.1 = ((bf16[12,2,64,256]{3,1,0,2:T(2,128)(2,1)}), bf16[12,2,64,256]{3,1,0,2:T(2,128)(2,1)S(1)}, u32[]{:S(2)}, u32[]{:S(2)}) async-start(bf16[12,2,64,256]{3,1,0,2:T(2,128)(2,1)} %copy.50), calls=%async_computation.1 | async-start | bytes 1572864 | tf_op jit(solution)/shard_map/all_to_all | solution.py:75
  244.0 248.8 %reduce-scatter.2.cloned.1.call-start = ((), (), s32[]{:S(2)}) async-start(), calls=%async_computation.6 | async-start | bytes 4718592 | tf_op jit(solution)/shard_map/reduce_scatter | solution.py:95
  250.7 1.2 copy-start.3
  253.5 4.5 copy-start.6
  258.0 6.0 %copy-start.5 = (bf16[2048,384,1]{0,1,2:T(8,128)(2,1)S(1)}, bf16[2048,384,1]{0,1,2:T(8,128)(2,1)}, u32[]{:S(2)}) copy-start(bf16[2048,384,1]{0,1,2:T(8,128)(2,1)} %reshape.236) | copy-start | bytes 4718596
  262.0 2.0 copy-start.8
  284.2 12.6 %slice-start.3 = ((s8[12582912]{0:T(1024)(128)(4,1)}), s8[4194304]{0:T(1024)(128)(4,1)S(1)}, s32[]{:S(2)}) async-start(s8[12582912]{0:T(1024)(128)(4,1)} %bitcast.130), calls=%async_computation.10 | async-start | bytes 8388608
  288.4 8.4 %slice-start.4 = ((s8[12582912]{0:T(1024)(128)(4,1)}), s8[4194304]{0:T(1024)(128)(4,1)S(1)}, s32[]{:S(2)}) async-start(s8[12582912]{0:T(1024)(128)(4,1)} %bitcast.130), calls=%async_computation.11 | async-start | bytes 8388608
  292.5 4.3 slice-start.5
  409.8 82.9 %copy-start.7 = (s32[8,64]{1,0:T(8,128)S(1)}, s32[8,64]{1,0:T(8,128)}, u32[]{:S(2)}) copy-start(s32[8,64]{1,0:T(8,128)} %param.9) | copy-start | bytes 6148
  409.8 87.9 %copy-start.1 = (bf16[8,64,2048]{2,1,0:T(8,128)(2,1)S(1)}, bf16[8,64,2048]{2,1,0:T(8,128)(2,1)}, u32[]{:S(2)}) copy-start(bf16[8,64,2048]{2,1,0:T(8,128)(2,1)} %param.5) | copy-start | bytes 6291460
Sparse Core Ops, SparseCore 0:
  24.9 100.8 all-gather.1
  409.9 82.7 reduce-scatter.1
where the time goes:
time: 512 us; the launch traced here: 505 us
  waiting for transfers between devices  223 us (44%)
  local copies, waits for them, and re-layouts  133 us (26%)
  blocking collectives  60.3 us (12%)
  matrix products  44.7 us (9%)
  other arithmetic  15.6 us (3%)
  between operations  14.6 us (3%)
  starting transfers between devices  14.1 us (3%)
    all_gather x1, waiting for transfers between devices, local(): everyone = lax.all_gather(bins_local, 'src', axis=2, tiled=True)  101 us
    reduce_scatter x1, waiting for transfers between devices, local(): lax.psum_scatter(moved, 'src', scatter_dimension=0, tiled=True)  82.9 us
    unnamed x34, local copies, waits for them, and re-layouts  53.3 us
    all_to_all x1, blocking collectives, local(): lax.all_to_all(partial_terms, 'freq', split_axis=3, concat_axis=1, tiled=...  43.4 us
    all_to_all x1, waiting for transfers between devices, local(): lax.all_to_all(everyone, 'freq', split_axis=0, concat_axis=3, tiled=True)  37 us
    all_to_all x2, local copies, waits for them, and re-layouts, local(): lax.all_to_all(partial_terms, 'freq', split_axis=3, concat_axis=1, tiled=...  25.4 us
    all_to_all x2, local copies, waits for them, and re-layouts, local(): lax.all_to_all(everyone, 'freq', split_axis=0, concat_axis=3, tiled=True)  21 us
    all_to_all x1, blocking collectives, local(): lax.all_to_all(back_local, 'freq', split_axis=0, concat_axis=2, tiled=True)  16.9 us
  transfers between devices with their start and end apart: 4, of which 4 were waited for; matrix products, arithmetic and copies ran while one was open for 2% of the time, Pallas kernels for 0%

commit v1 on v0

--- a/solution.py
+++ b/solution.py
@@ -66,7 +66,9 @@
         "tk,prt->kpr", forward_table, focusing, preferred_element_type=jnp.float32
     )
     bins_local = bins_local.astype(jnp.bfloat16).reshape(NF, 2, point_count, recv_count)
-    everyone = lax.all_gather(bins_local, "src", axis=2, tiled=True)
+    everyone = jnp.concatenate(
+        lax.all_to_all(jnp.stack([bins_local] * lax.axis_size("src")), "src", 0, 0), axis=2
+    )
     waves = forward_waves(
         kernel_real_part,
         kernel_imaginary,

time: 512 us -> 482 us (0.941)
  waiting for transfers between devices: 223 us -> 121 us
  blocking collectives: 60.3 us -> 119 us
  local copies, waits for them, and re-layouts: 133 us -> 144 us
    all_gather x1 -> x0, waiting for transfers between devices: 101 us -> none  [local(): everyone = lax.all_gather(bins_local, 'src', axis=2, tiled=True)]
    all_to_all x0 -> x1, blocking collectives: none -> 58.5 us  [local(): lax.all_to_all(jnp.stack([bins_local] * lax.axis_size('src')), 'src', 0, 0)]
    reshape x0 -> x1, local copies, waits for them, and re-layouts: none -> 9.11 us  [local(): jnp.concatenate(lax.all_to_all(jnp.stack([bins_local] * lax.axis_size('sr...]
  transfers between devices with their start and end apart: 4 -> 3, of which waited for: 4 -> 3; matrix products, arithmetic and copies ran while one was open for 2% -> 3% of each run, Pallas kernels for 0% -> 0%
where the time goes in v1:
time: 482 us; the launch traced here: 473 us
  local copies, waits for them, and re-layouts  144 us (30%)
  waiting for transfers between devices  121 us (25%)
  blocking collectives  119 us (25%)
  matrix products  44.7 us (9%)
  other arithmetic  15.6 us (3%)
  between operations  14.6 us (3%)
  starting transfers between devices  14.4 us (3%)
    reduce_scatter x1, waiting for transfers between devices, local(): lax.psum_scatter(moved, 'src', scatter_dimension=0, tiled=True)  82 us
    all_to_all x1, blocking collectives, local(): lax.all_to_all(jnp.stack([bins_local] * lax.axis_size('src')), 'src', 0, 0)  58.5 us
    unnamed x34, local copies, waits for them, and re-layouts  53.3 us
    all_to_all x1, blocking collectives, local(): lax.all_to_all(partial_terms, 'freq', split_axis=3, concat_axis=1, tiled=...  43.4 us
    all_to_all x1, waiting for transfers between devices, local(): lax.all_to_all(everyone, 'freq', split_axis=0, concat_axis=3, tiled=True)  37 us
    all_to_all x2, local copies, waits for them, and re-layouts, local(): lax.all_to_all(partial_terms, 'freq', split_axis=3, concat_axis=1, tiled=...  25.4 us
    all_to_all x2, local copies, waits for them, and re-layouts, local(): lax.all_to_all(everyone, 'freq', split_axis=0, concat_axis=3, tiled=True)  20.9 us
    all_to_all x1, blocking collectives, local(): lax.all_to_all(back_local, 'freq', split_axis=0, concat_axis=2, tiled=True)  16.9 us
  transfers between devices with their start and end apart: 3, of which 3 were waited for; matrix products, arithmetic and copies ran while one was open for 3% of the time, Pallas kernels for 0%

profile of v1, /device:TPU:0, one launch (start us, length us, event | category | flops | bytes accessed | tf_op | source)
XLA Modules:
  0.0 473.4 jit_solution(16305402035372880446)
XLA Ops:
  7.2 6.9 %cosine_convert_fusion = (bf16[2048,192,1]{0,1,2:T(8,128)(2,1)S(1)}, bf16[2048,192,1]{0,1,2:T(8,128)(2,1)S(1)}) fusion(s32[192]{0:T(256)S(1)} %iota_add_fusion), kind=kLoop, calls=%fused_computation.57 | loop fusion | flops 6684672 | bytes 1573632 | tf_op jit(solution)/shard_map/convert.10
  25.1 58.5 %all_to_all.74 = bf16[8,192,2,8,64]{1,4,3,2,0:T(8,128)(2,1)S(1)} all-to-all(bf16[8,192,2,8,64]{1,4,3,2,0:T(8,128)(2,1)S(1)} %stack.39), channel_id=1, replica_groups=mesh['freq'=16,'src'=8] {'src'}, dimensions={0} | all-to-all | bytes 6291456 | tf_op jit(solution)/shard_map/all_to_all | solution.py:70
  85.8 9.1 %copy.59 = bf16[192,2,64,64]{3,2,1,0:T(8,128)(2,1)} copy(bf16[192,2,64,64]{0,3,2,1:T(8,128)(2,1)} %bitcast.139) | data formatting | bytes 6291456 | tf_op jit(solution)/shard_map/reshape | solution.py:69
  95.0 12.7 %reshape.247 = bf16[16,2,49152]{2,1,0:T(2,128)(2,1)} reshape(bf16[192,2,64,64]{3,2,1,0:T(8,128)(2,1)} %copy.59) | data formatting | bytes 6291456
  107.6 5.3 %all-to-all-start.1 = ((bf16[16,2,49152]{2,1,0:T(2,128)(2,1)}), bf16[16,2,49152]{2,1,0:T(2,128)(2,1)}, u32[]{:S(2)}, u32[]{:S(2)}) async-start(bf16[16,2,49152]{2,1,0:T(2,128)(2,1)} %reshape.247), calls=%async_computation.1 | async-start | bytes 6291456 | tf_op jit(solution)/shard_map/all_to_all | solution.py:75
  115.0 37.0 %all-to-all-done.1 = bf16[16,2,49152]{2,1,0:T(2,128)(2,1)} async-done(((bf16[16,2,49152]{2,1,0:T(2,128)(2,1)}), bf16[16,2,49152]{2,1,0:T(2,128)(2,1)}, u32[]{:S(2)}, u32[]{:S(2)}) %all-to-all-start.1) | async-done | bytes 3145760 | tf_op jit(solution)/shard_map/all_to_all | solution.py:75
  152.0 12.3 %reshape.248 = bf16[192,2,64,64]{3,2,1,0:T(8,128)(2,1)} reshape(bf16[16,2,49152]{2,1,0:T(2,128)(2,1)} %all-to-all-done.1) | data formatting | bytes 6291456
  164.3 11.1 %copy.60 = bf16[12,2,64,16,64]{4,3,2,0,1:T(8,128)(2,1)} copy(bf16[12,2,64,16,64]{4,2,1,0,3:T(8,128)(2,1)} %bitcast.135) | data formatting | bytes 6291456 | tf_op jit(solution)/shard_map/all_to_all | solution.py:75
  175.3 9.9 %all_to_all.57 = bf16[12,2,64,1024]{3,2,0,1:T(8,128)(2,1)} reshape(bf16[12,2,64,16,64]{4,3,2,0,1:T(8,128)(2,1)} %copy.60) | data formatting | bytes 6291456 | tf_op jit(solution)/shard_map/all_to_all | solution.py:75
  185.3 5.4 %fusion.4 = f32[12,64,256]{2,1,0:T(8,128)S(1)} fusion(bf16[2,12,256,1024]{3,2,1,0:T(8,128)(2,1)} %param.7, bf16[12,2,64,1024]{3,2,0,1:T(8,128)(2,1)} %all_to_all.57), kind=kOutput, calls=%fused_computation.6 | convolution fusion | flops 402653184 | bytes 8650752 | tf_op jit(solution)/shard_map/izb,ijb->ijz/dot_general | solution.py:36
  190.7 5.0 %fusion.6 = f32[12,64,256]{2,1,0:T(8,128)S(1)} fusion(bf16[2,12,256,1024]{3,2,1,0:T(8,128)(2,1)} %param.7, bf16[12,2,64,1024]{3,2,0,1:T(8,128)(2,1)S(1)} %copy-done.4), kind=kOutput, calls=%fused_computation.8 | convolution fusion | flops 402653184 | bytes 8650752 | tf_op jit(solution)/shard_map/izb,ijb->ijz/dot_general | solution.py:31
  195.7 5.0 %fusion.70 = bf16[12,1,64,256]{3,2,0,1:T(8,128)(2,1)S(1)} fusion(f32[12,64,256]{2,1,0:T(8,128)S(1)} %fusion.4, bf16[2,12,256,1024]{3,2,1,0:T(8,128)(2,1)} %param.7, bf16[12,2,64,1024]{3,2,0,1:T(8,128)(2,1)S(1)} %copy-done.4), kind=kOutput, calls=%fused_computation.71 | convolution fusion | flops 403046400 | bytes 9043968 | tf_op jit(solution)/shard_map/izb,ijb->ijz/dot_general | solution.py:34
  204.6 8.9 %all-to-all-start.2 = ((bf16[12,2,64,256]{3,1,0,2:T(2,128)(2,1)}), bf16[12,2,64,256]{3,1,0,2:T(2,128)(2,1)S(1)}, u32[]{:S(2)}, u32[]{:S(2)}) async-start(bf16[12,2,64,256]{3,1,0,2:T(2,128)(2,1)} %copy.61), calls=%async_computation.2 | async-start | bytes 1572864 | tf_op jit(solution)/shard_map/all_to_all | solution.py:77
  213.7 6.2 %fusion.74 = (f32[192,1,2048]{2,0,1:T(8,128)S(1)}, f32[192,1,2048]{2,0,1:T(8,128)S(1)}) fusion(s32[192]{0:T(256)S(1)} %iota_add_fusion), kind=kLoop, calls=%fused_computation.75 | loop fusion | flops 5898240 | bytes 3146496 | tf_op jit(solution)/shard_map/cos | solution.py:17
  236.3 16.9 %all_to_all.75 = bf16[192,2,4,256]{3,1,2,0:T(2,128)(2,1)S(1)} all-to-all(bf16[192,2,4,256]{3,1,2,0:T(2,128)(2,1)S(1)} %copy.65), channel_id=1, replica_groups=mesh['freq'=16,'src'=8] {'freq'}, dimensions={0} | all-to-all | bytes 1572864 | tf_op jit(solution)/shard_map/all_to_all | solution.py:93
  262.1 4.2 fusion.49
  269.6 15.9 %copy.67 = bf16[64,12,2,1024]{0,2,1,3:T(2,128)(2,1)} copy(bf16[64,12,2,1024]{3,0,1,2:T(8,128)(2,1)} %pad_maximum_fusion) | data formatting | bytes 6291456 | tf_op jit(solution)/shard_map/stack | solution.py:55
  285.5 12.7 %reshape.249 = bf16[16,2,49152]{2,1,0:T(2,128)(2,1)} reshape(bf16[1024,12,2,64]{3,2,1,0:T(2,128)(2,1)} %bitcast.136) | data formatting | bytes 6291456
  298.2 43.4 %all_to_all.76 = bf16[16,2,49152]{2,1,0:T(2,128)(2,1)} all-to-all(bf16[16,2,49152]{2,1,0:T(2,128)(2,1)} %reshape.249), channel_id=1, replica_groups=mesh['freq'=16,'src'=8] {'freq'}, dimensions={0} | all-to-all | bytes 6291456 | tf_op jit(solution)/shard_map/all_to_all | solution.py:95
  341.6 12.3 %reshape.250 = bf16[1024,12,2,64]{3,2,1,0:T(2,128)(2,1)} reshape(bf16[16,2,49152]{2,1,0:T(2,128)(2,1)} %all_to_all.76) | data formatting | bytes 6291456
  353.9 16.3 %copy.68 = bf16[64,12,2,16,64]{4,0,2,1,3:T(8,128)(2,1)} copy(bf16[64,12,2,16,64]{0,2,1,4,3:T(2,128)(2,1)} %bitcast.137) | data formatting | bytes 6291456 | tf_op jit(solution)/shard_map/all_to_all | solution.py:95
  370.1 9.1 %copy.69 = bf16[64,192,2,64]{1,3,2,0:T(8,128)(2,1)} copy(bf16[64,192,2,64]{3,0,2,1:T(8,128)(2,1)} %bitcast.138) | data formatting | bytes 6291456 | tf_op jit(solution)/shard_map/all_to_all | solution.py:95
  379.3 82.0 %reduce-scatter.2.cloned.1.call-done = bf16[8,192,2,64]{1,3,2,0:T(8,128)(2,1)} async-done(((bf16[64,192,2,64]{1,3,2,0:T(8,128)(2,1)}), bf16[8,192,2,64]{1,3,2,0:T(8,128)(2,1)}) %reduce-scatter.2.cloned.1.call-update) | async-done | bytes 393232 | tf_op jit(solution)/shard_map/reduce_scatter | solution.py:97
  461.3 5.0 %fusion.17 = bf16[8,64,2048]{2,1,0:T(8,128)(2,1)} fusion(bf16[8,64,2048]{2,1,0:T(8,128)(2,1)} %param.6, bf16[8,192,2,64]{1,3,2,0:T(8,128)(2,1)} %reduce-scatter.2.cloned.1.call-done, s32[8,64]{1,0:T(8,128)S(1)} %copy-done.7, bf16[192,2,2048]{2,0,1:T(8,128)(2,1)} %copy-done.3), kind=kOutput, calls=%fused_computation.20 | convolution fusion | flops 810549248 | bytes 6162432 | tf_op jit(solution)/shard_map/pkr,kt->prt/dot_general | solution.py:102
  (62 shorter events, 47.6 us)
Async XLA Ops:
  7.2 13.5 %copy-start = (bf16[8,64,2048]{2,1,0:T(8,128)(2,1)S(1)}, bf16[8,64,2048]{2,1,0:T(8,128)(2,1)}, u32[]{:S(2)}) copy-start(bf16[8,64,2048]{2,1,0:T(8,128)(2,1)} %param.5) | copy-start | bytes 6291460
  107.6 5.4 %copy-start.2 = (bf16[2048,192,2]{0,2,1:T(2,128)(2,1)S(1)}, bf16[2048,192,2]{0,2,1:T(2,128)(2,1)}, u32[]{:S(2)}) copy-start(bf16[2048,192,2]{0,2,1:T(2,128)(2,1)} %copy.54) | copy-start | bytes 4718596
  107.6 44.3 %all-to-all-start.1 = ((bf16[16,2,49152]{2,1,0:T(2,128)(2,1)}), bf16[16,2,49152]{2,1,0:T(2,128)(2,1)}, u32[]{:S(2)}, u32[]{:S(2)}) async-start(bf16[16,2,49152]{2,1,0:T(2,128)(2,1)} %reshape.247), calls=%async_computation.1 | async-start | bytes 6291456 | tf_op jit(solution)/shard_map/all_to_all | solution.py:75
  185.2 5.5 %copy-start.4 = (bf16[12,2,64,1024]{3,2,0,1:T(8,128)(2,1)S(1)}, bf16[12,2,64,1024]{3,2,0,1:T(8,128)(2,1)}, u32[]{:S(2)}) copy-start(bf16[12,2,64,1024]{3,2,0,1:T(8,128)(2,1)} %all_to_all.57) | copy-start | bytes 9437188
  185.2 15.5 %slice-start = ((s8[12582912]{0:T(1024)(128)(4,1)}), s8[4194304]{0:T(1024)(128)(4,1)S(1)}, s32[]{:S(2)}) async-start(s8[12582912]{0:T(1024)(128)(4,1)} %bitcast.131), calls=%async_computation.7 | async-start | bytes 8388608
  190.7 10.1 %slice-start.1 = ((s8[12582912]{0:T(1024)(128)(4,1)}), s8[4194304]{0:T(1024)(128)(4,1)S(1)}, s32[]{:S(2)}) async-start(s8[12582912]{0:T(1024)(128)(4,1)} %bitcast.131), calls=%async_computation.8 | async-start | bytes 8388608
  195.7 5.1 %slice-start.2 = ((s8[12582912]{0:T(1024)(128)(4,1)}), s8[4194304]{0:T(1024)(128)(4,1)S(1)}, s32[]{:S(2)}) async-start(s8[12582912]{0:T(1024)(128)(4,1)} %bitcast.131), calls=%async_computation.9 | async-start | bytes 8388608
  204.6 22.5 %all-to-all-start.2 = ((bf16[12,2,64,256]{3,1,0,2:T(2,128)(2,1)}), bf16[12,2,64,256]{3,1,0,2:T(2,128)(2,1)S(1)}, u32[]{:S(2)}, u32[]{:S(2)}) async-start(bf16[12,2,64,256]{3,1,0,2:T(2,128)(2,1)} %copy.61), calls=%async_computation.2 | async-start | bytes 1572864 | tf_op jit(solution)/shard_map/all_to_all | solution.py:77
  213.5 247.8 %reduce-scatter.2.cloned.1.call-start = ((), (), s32[]{:S(2)}) async-start(), calls=%async_computation.6 | async-start | bytes 4718592 | tf_op jit(solution)/shard_map/reduce_scatter | solution.py:97
  220.2 1.2 copy-start.3
  223.0 4.5 copy-start.6
  227.6 6.0 %copy-start.5 = (bf16[2048,384,1]{0,1,2:T(8,128)(2,1)S(1)}, bf16[2048,384,1]{0,1,2:T(8,128)(2,1)}, u32[]{:S(2)}) copy-start(bf16[2048,384,1]{0,1,2:T(8,128)(2,1)} %reshape.242) | copy-start | bytes 4718596
  231.6 2.0 copy-start.8
  253.8 12.6 %slice-start.3 = ((s8[12582912]{0:T(1024)(128)(4,1)}), s8[4194304]{0:T(1024)(128)(4,1)S(1)}, s32[]{:S(2)}) async-start(s8[12582912]{0:T(1024)(128)(4,1)} %bitcast.133), calls=%async_computation.10 | async-start | bytes 8388608
  257.9 8.4 %slice-start.4 = ((s8[12582912]{0:T(1024)(128)(4,1)}), s8[4194304]{0:T(1024)(128)(4,1)S(1)}, s32[]{:S(2)}) async-start(s8[12582912]{0:T(1024)(128)(4,1)} %bitcast.133), calls=%async_computation.11 | async-start | bytes 8388608
  262.1 4.3 slice-start.5
  379.2 82.1 %copy-start.7 = (s32[8,64]{1,0:T(8,128)S(1)}, s32[8,64]{1,0:T(8,128)}, u32[]{:S(2)}) copy-start(s32[8,64]{1,0:T(8,128)} %param.9) | copy-start | bytes 6148
  379.3 87.1 %copy-start.1 = (bf16[8,64,2048]{2,1,0:T(8,128)(2,1)S(1)}, bf16[8,64,2048]{2,1,0:T(8,128)(2,1)}, u32[]{:S(2)}) copy-start(bf16[8,64,2048]{2,1,0:T(8,128)(2,1)} %param.5) | copy-start | bytes 6291460
Sparse Core Ops, SparseCore 0:
  379.4 81.8 reduce-scatter.1
